TPU v7x, 32 devices: a whole 2x2x4 slice. The times are simulated.
32 devices in a mesh: groups: 2 (over y), coef: 4 (over x, core), slab: 4 (over z).
Axes of the slice: x: 2, y: 2, z: 4, core: 2. Of those that a mesh axis runs over, the one named last changes fastest.
Arguments:
- coefficients: float32 [896, 32768], P('coef', ('groups', 'slab')), parts along dimension 1, may hold values from -6 to 6
- measured: float32 [16, 4, 64, 256], P('groups', 'slab'), parts along dimension 0, may hold values from -6 to 6
- ray_voxels: int32 [8, 64, 128], replicated, may hold values from 0 to 4095
- ray_weights: int32 [8, 64, 128], replicated, may hold values from 1 to 63
- angle_ids: int32 [8], replicated, may hold values from 0 to 15
- angle_table: bfloat16 [16, 896, 256], P(None, 'coef'), may hold values from -0.1875 to 0.1875
- harmonics: bfloat16 [896, 2048], P('coef'), may hold values from -0.1875 to 0.1875
Outputs:
- updated: float32 [896, 32768], P('coef', ('groups', 'slab')), parts along dimension 1
- residual: float32 [16, 4, 64, 256], P('groups', 'slab', None, 'coef'), parts along dimension 0
There are 2 independent parts, one for each index of `groups`. A program takes and returns all parts, laid end to end along the dimension named above; an argument that names none is the same for every part. Nothing has to cross between parts.
All inputs are finite; a program needn't handle non-finite values.
Results may differ from a plain program's by a relative error of at most 0.0034.
Values may be sent and summed in bfloat16 or wider, within the bound.
A program may use at most 64 MiB of HBM per device.

v0:
```python
import jax
import jax.numpy as jnp
from jax import lax
from jax.sharding import PartitionSpec as P

NG = 64


def build_matrix(ray_voxels, ray_weights):
    shape_all = ray_voxels.shape
    side_count = NG
    high_part = ray_voxels // side_count
    low_part = ray_voxels % side_count
    positions = jnp.arange(side_count, dtype=jnp.int32)
    values = (ray_weights.astype(jnp.float32) / 256.0).astype(jnp.bfloat16)
    high_table = jnp.where(
        high_part[..., None] == positions, values[..., None], jnp.zeros((), jnp.bfloat16)
    )
    low_table = (low_part[..., None] == positions).astype(jnp.bfloat16)
    high_flat = high_table.reshape(shape_all[0] * shape_all[1], shape_all[2], side_count)
    low_flat = low_table.reshape(shape_all[0] * shape_all[1], shape_all[2], side_count)
    product = lax.dot_general(
        high_flat, low_flat, (((1,), (1,)), ((0,), (0,))), preferred_element_type=jnp.float32
    )
    return product.astype(jnp.bfloat16).reshape(shape_all[0], shape_all[1], side_count * side_count)


def select_angles(angle_ids, angle_table):
    entries = angle_table.shape[0]
    onehot = (angle_ids[:, None] == jnp.arange(entries)[None, :]).astype(jnp.bfloat16)
    flat_table = angle_table.reshape(entries, -1)
    picked = jnp.dot(onehot, flat_table, preferred_element_type=jnp.float32)
    return picked.astype(jnp.bfloat16).reshape((angle_ids.shape[0],) + angle_table.shape[1:])


def body(coefficients, measured, ray_voxels, ray_weights, angle_ids, angle_table, harmonics):
    coef_local = coefficients.shape[0]
    layers = coefficients.shape[1] // (NG * NG)
    system_matrix = build_matrix(ray_voxels, ray_weights)
    chosen = select_angles(angle_ids, angle_table)
    coef_half = coefficients.astype(jnp.bfloat16)
    stacked_rows = coef_half.reshape(coef_local, layers, NG * NG)
    ray_totals = jnp.einsum(
        "dmj,hqj->dqmh", system_matrix, stacked_rows, preferred_element_type=jnp.float32
    ).astype(jnp.bfloat16)
    partial_value = jnp.einsum(
        "azrk,akc->azrc", ray_totals, chosen, preferred_element_type=jnp.float32
    )
    chan_width = measured.shape[3] // lax.axis_size("coef")
    chan_start = lax.axis_index("coef") * chan_width
    predicted = lax.psum_scatter(partial_value, "coef", scatter_dimension=3, tiled=True)
    residual = predicted - lax.dynamic_slice_in_dim(measured, chan_start, chan_width, 3)
    resid_half = residual.astype(jnp.bfloat16)
    backward_projection = jnp.einsum(
        "azrc,akc->azrk",
        lax.all_gather(resid_half, "coef", axis=3, tiled=True),
        chosen,
        preferred_element_type=jnp.float32,
    )
    backward_half = backward_projection.astype(jnp.bfloat16)
    misfit_gradient = jnp.einsum(
        "qci,qbcy->ybi", system_matrix, backward_half, preferred_element_type=jnp.float32
    )
    misfit_gradient = misfit_gradient.reshape(coef_local, layers * NG * NG)
    grid_rows = coef_half.reshape(coef_local, layers * NG, NG)
    blocks = lax.all_to_all(grid_rows, "coef", split_axis=1, concat_axis=0, tiled=True)
    width_all, row_span, item_count = blocks.shape
    flat_cols = blocks.reshape(width_all, row_span * item_count)
    orient_field = lax.dot_general(
        flat_cols,
        lax.all_gather(harmonics, "coef", axis=0, tiled=True),
        (((0,), (0,)), ((), ())),
        preferred_element_type=jnp.float32,
    )
    slope_half = (-jax.nn.sigmoid(-orient_field)).astype(jnp.bfloat16)
    reg_grad = lax.dot_general(
        lax.all_gather(harmonics, "coef", axis=0, tiled=True),
        slope_half,
        (((1,), (1,)), ((), ())),
        preferred_element_type=jnp.float32,
    )
    reg_grad = reg_grad.reshape(width_all, row_span, item_count)
    reg_grad = lax.all_to_all(reg_grad, "coef", split_axis=0, concat_axis=1, tiled=True)
    reg_grad = reg_grad.reshape(coef_local, layers * NG * NG)
    updated = coefficients - 0.5 * misfit_gradient - 0.5 * reg_grad
    return (updated, residual)


def solution(mesh):
    in_specs = (
        P("coef", ("groups", "slab")),
        P("groups", "slab", None, None),
        P(),
        P(),
        P(),
        P(None, "coef", None),
        P("coef", None),
    )
    out_specs = (P("coef", ("groups", "slab")), P("groups", "slab", None, "coef"))
    return jax.shard_map(body, mesh=mesh, in_specs=in_specs, out_specs=out_specs, check_vma=False)
```

profile of v0, /device:TPU:0, one launch (start us, length us, event | category | flops | bytes accessed | tf_op | source)
XLA Modules:
  0.0 229.0 jit_solution(1820628051874065335)
XLA Ops:
  7.2 0.0 all-gather.2.cloned.1.call-start
  7.2 0.7 all-gather.2.cloned.1.call-update
  7.9 2.3 convert_element_type.36
  10.2 0.0 copy-start
  10.2 0.0 copy-start.3
  10.2 0.0 copy-start.2
  10.2 2.5 %copy.37 = bf16[224,4096]{0,1:T(8,128)(2,1)} copy(bf16[224,4096]{1,0:T(8,128)(2,1)S(1)} %convert_element_type.36) | data formatting | bytes 3670016 | tf_op jit(solution)/shard_map/convert_element_type | solution.py:41
  12.7 0.0 copy-done
  12.7 4.2 %all-to-all-start = ((bf16[224,64,64]{0,2,1:T(8,128)(2,1)}), bf16[224,64,64]{0,2,1:T(8,128)(2,1)S(1)}, u32[]{:S(2)}, u32[]{:S(2)}) async-start(bf16[224,64,64]{0,2,1:T(8,128)(2,1)} %bitcast.58), calls=%async_computation | async-start | bytes 4194304 | tf_op jit(solution)/shard_map/all_to_all | solution.py:66
  16.9 0.0 copy-done.3
  17.0 0.0 copy-done.2
  17.0 0.2 add_select_fusion.1
  17.2 45.1 %all-to-all-done = bf16[224,64,64]{0,2,1:T(8,128)(2,1)S(1)} async-done(((bf16[224,64,64]{0,2,1:T(8,128)(2,1)}), bf16[224,64,64]{0,2,1:T(8,128)(2,1)S(1)}, u32[]{:S(2)}, u32[]{:S(2)}) %all-to-all-start) | async-done | bytes 1835040 | tf_op jit(solution)/shard_map/all_to_all | solution.py:66
  62.3 3.1 %copy.53 = bf16[224,4,16,64]{0,1,3,2:T(4,128)(2,1)} copy(bf16[224,4,16,64]{0,3,2,1:T(8,128)(2,1)S(1)} %bitcast.57) | data formatting | bytes 3670016 | tf_op jit(solution)/shard_map/all_to_all | solution.py:66
  65.3 3.9 %reshape.62 = bf16[896,1024]{0,1:T(8,128)(2,1)S(1)} reshape(bf16[4,224,16,64]{1,0,3,2:T(4,128)(2,1)} %bitcast.59) | data formatting | bytes 3670016 | tf_op jit(solution)/shard_map/reshape | solution.py:68
  69.3 0.0 all-gather.2.cloned.1.call-done
  69.3 13.8 %fusion.13 = f32[1024,896]{1,0:T(8,128)} fusion(bf16[896,2048]{1,0:T(8,128)(2,1)} %all-gather.2.cloned.1.call-done, bf16[896,1024]{0,1:T(8,128)(2,1)S(1)} %reshape.62), kind=kOutput, calls=%fused_computation.15 | convolution fusion | flops 7524581376 | bytes 9175040 | tf_op jit(solution)/shard_map/dot_general | solution.py:76
  83.1 7.7 %copy.39 = f32[896,16,64]{2,1,0:T(8,128)} copy(f32[896,16,64]{0,2,1:T(8,128)} %bitcast.64) | data formatting | bytes 7340032 | tf_op jit(solution)/shard_map/reshape | solution.py:82
  90.8 7.8 %reshape.68 = f32[4,1,229376]{2,1,0:T(1,128)} reshape(f32[896,16,64]{2,1,0:T(8,128)} %copy.39) | data formatting | bytes 7340032
  98.6 4.8 %all-to-all-start.1 = ((f32[4,1,229376]{2,1,0:T(1,128)}), f32[4,1,229376]{2,1,0:T(1,128)}, u32[]{:S(2)}, u32[]{:S(2)}) async-start(f32[4,1,229376]{2,1,0:T(1,128)} %reshape.68), calls=%async_computation.1 | async-start | bytes 7340032 | tf_op jit(solution)/shard_map/all_to_all | solution.py:83
  103.4 0.2 reduce-scatter.4.cloned.1.call-start
  103.6 6.6 %fusion.5 = bf16[512,64,64]{2,1,0:T(8,128)(2,1)} fusion(s32[512,128]{1,0:T(8,128)S(1)} %bitcast.68, s32[512,128]{1,0:T(8,128)S(1)} %bitcast.67, bf16[512,128]{1,0:T(8,128)(2,1)S(1)} %bitcast.70), kind=kOutput, calls=%fused_computation.8 | convolution fusion | flops 551550976 | bytes 4849664 | tf_op jit(solution)/shard_map/dot_general | solution.py:22
  110.3 12.0 %reshape.57 = bf16[8,64,4096]{2,1,0:T(8,128)(2,1)} reshape(bf16[512,64,64]{2,1,0:T(8,128)(2,1)} %fusion.5) | data formatting | bytes 8388608 | tf_op jit(solution)/shard_map/reshape | solution.py:25
  122.3 0.0 copy-start.5
  122.3 0.0 copy-start.1
  122.3 2.7 %copy.46 = bf16[2,8,224,256]{3,1,2,0:T(8,128)(2,1)S(1)} copy(bf16[2,8,224,256]{3,2,1,0:T(8,128)(2,1)} %bitcast.65) | data formatting | bytes 3670016
  125.0 0.0 copy-done.5
  125.0 0.5 convolution_convert_fusion
  125.4 0.0 copy-done.1
  125.5 3.8 %convolution_bitcast_fusion.1 = f32[8,1,64,256]{3,2,0,1:T(8,128)S(1)} fusion(bf16[8,224,256]{2,0,1:T(8,128)(2,1)S(1)} %bitcast.62, bf16[8,64,4096]{2,1,0:T(8,128)(2,1)} %reshape.57, bf16[224,4096]{1,0:T(8,128)(2,1)S(1)} %copy-done.1), kind=kOutput, calls=%fused_computation.20 | convolution fusion | flops 998359040 | bytes 7471104 | tf_op jit(solution)/shard_map/azrk,akc->azrc/dot_general | solution.py:46
  129.3 0.0 copy-start.4
  129.3 0.4 copy.44
  129.7 1.1 reshape.66
  130.8 0.0 reduce-scatter.4.cloned.1.call-update
  130.8 24.1 %reduce-scatter.4.cloned.1.call-done = f32[64,512]{1,0:T(8,128)} async-done(((f32[256,512]{1,0:T(8,128)}), f32[64,512]{1,0:T(8,128)}) %reduce-scatter.4.cloned.1.call-update) | async-done | bytes 131088
  155.0 1.0 reshape.67
  156.0 0.1 copy.45
  156.1 0.0 copy-done.4
  156.1 0.8 fusion.28
  157.0 0.1 copy.34
  157.1 6.8 %all_gather.7 = bf16[8,1,64,256]{2,0,1,3:T(8,128)(2,1)S(1)} all-gather(bf16[8,1,64,64]{2,0,1,3:T(8,128)(2,1)S(1)} %copy.34), channel_id=1, replica_groups=mesh['groups'=2,'coef'=4,'slab'=4] {'coef'}, dimensions={3}, use_global_device_ids=true | all-gather | bytes 327680 | tf_op jit(solution)/shard_map/all_gather | solution.py:56
  163.9 0.3 copy.35
  164.2 0.0 all-to-all-done.1
  164.3 0.5 broadcast.44
  164.8 13.6 %reduce = f32[4,229376]{1,0:T(4,128)} reduce(f32[4,1,229376]{2,1,0:T(1,128)} %all-to-all-done.1, f32[]{:T(128)} %broadcast.44), dimensions={1}, to_apply=%all_to_all.21.reduce_sub_computation | reduce | bytes 7340036 | tf_op jit(solution)/shard_map/all_to_all | solution.py:83
  178.4 8.4 %reshape.69 = f32[896,16,64]{2,1,0:T(8,128)} reshape(f32[4,229376]{1,0:T(4,128)} %reduce) | data formatting | bytes 7340032
  186.8 6.5 %copy.40 = f32[896,16,64]{0,2,1:T(8,128)} copy(f32[896,16,64]{2,1,0:T(8,128)} %reshape.69) | data formatting | bytes 7340032 | tf_op jit(solution)/shard_map/all_to_all | solution.py:83
  193.3 4.2 %broadcast_multiply_fusion = f32[896,16,64]{0,2,1:T(8,128)} fusion(f32[896,16,64]{0,2,1:T(8,128)} %copy.40), kind=kLoop, calls=%fused_computation.19 | loop fusion | flops 917504 | bytes 7340032 | tf_op jit(solution)/shard_map/mul | solution.py:85
  197.6 6.4 %mul.21 = f32[4,224,16,64]{1,0,3,2:T(4,128)} reshape(f32[896,16,64]{0,2,1:T(8,128)} %broadcast_multiply_fusion) | data formatting | bytes 7340032 | tf_op jit(solution)/shard_map/mul | solution.py:85
  204.0 5.0 %copy.41 = f32[224,4,16,64]{0,3,2,1:T(8,128)} copy(f32[224,4,16,64]{0,1,3,2:T(4,128)} %bitcast.55) | data formatting | bytes 7340032 | tf_op jit(solution)/shard_map/mul | solution.py:85
  209.0 5.5 %copy.42 = f32[224,4096]{1,0:T(8,128)} copy(f32[224,4096]{0,1:T(8,128)} %bitcast.56) | data formatting | bytes 7340032 | tf_op jit(solution)/shard_map/mul | solution.py:85
  214.4 7.8 %fusion.10 = f32[224,4096]{1,0:T(8,128)} fusion(f32[224,4096]{1,0:T(8,128)} %copy.42, f32[224,4096]{1,0:T(8,128)} %param.7, bf16[8,64,4096]{2,1,0:T(8,128)(2,1)} %reshape.57, bf16[8,224,256]{2,0,1:T(8,128)(2,1)S(1)} %bitcast.63, bf16[8,1,64,256]{3,2,0,1:T(8,128)(2,1)S(1)} %copy.35), kind=kOutput, calls=%fused_computation.12 | convolution fusion | flops 1001111552 | bytes 16384000 | tf_op jit(solution)/shard_map/qci,qbcy->ybi/dot_general | solution.py:61
  (1 shorter events, 0.0 us)
Async XLA Ops:
  7.2 62.1 %all-gather.2.cloned.1.call-start = ((), (), s32[]{:S(2)}) async-start(), calls=%async_computation.3 | async-start | bytes 4587520 | tf_op jit(solution)/shard_map/all_gather | solution.py:77
  10.2 2.5 %copy-start = (bf16[224,4096]{1,0:T(8,128)(2,1)}, bf16[224,4096]{1,0:T(8,128)(2,1)S(1)}, u32[]{:S(2)}) copy-start(bf16[224,4096]{1,0:T(8,128)(2,1)S(1)} %convert_element_type.36) | copy-start | bytes 5505028
  10.2 6.7 %copy-start.3 = (s32[8,64,128]{2,1,0:T(8,128)S(1)}, s32[8,64,128]{2,1,0:T(8,128)}, u32[]{:S(2)}) copy-start(s32[8,64,128]{2,1,0:T(8,128)} %param.10) | copy-start | bytes 786436
  10.2 6.8 %copy-start.2 = (s32[8,64,128]{2,1,0:T(8,128)S(1)}, s32[8,64,128]{2,1,0:T(8,128)}, u32[]{:S(2)}) copy-start(s32[8,64,128]{2,1,0:T(8,128)} %param.9) | copy-start | bytes 786436
  12.7 49.6 %all-to-all-start = ((bf16[224,64,64]{0,2,1:T(8,128)(2,1)}), bf16[224,64,64]{0,2,1:T(8,128)(2,1)S(1)}, u32[]{:S(2)}, u32[]{:S(2)}) async-start(bf16[224,64,64]{0,2,1:T(8,128)(2,1)} %bitcast.58), calls=%async_computation | async-start | bytes 4194304 | tf_op jit(solution)/shard_map/all_to_all | solution.py:66
  98.6 65.7 %all-to-all-start.1 = ((f32[4,1,229376]{2,1,0:T(1,128)}), f32[4,1,229376]{2,1,0:T(1,128)}, u32[]{:S(2)}, u32[]{:S(2)}) async-start(f32[4,1,229376]{2,1,0:T(1,128)} %reshape.68), calls=%async_computation.1 | async-start | bytes 7340032 | tf_op jit(solution)/shard_map/all_to_all | solution.py:83
  103.4 51.6 %reduce-scatter.4.cloned.1.call-start = ((), (), s32[]{:S(2)}) async-start(), calls=%async_computation.4 | async-start | bytes 655360
  122.3 2.7 %copy-start.5 = (s32[8]{0:T(128)S(1)}, s32[8]{0:T(128)}, u32[]{:S(2)}) copy-start(s32[8]{0:T(128)} %param.11) | copy-start | bytes 100
  122.3 3.1 %copy-start.1 = (bf16[224,4096]{1,0:T(8,128)(2,1)S(1)}, bf16[224,4096]{1,0:T(8,128)(2,1)}, u32[]{:S(2)}) copy-start(bf16[224,4096]{1,0:T(8,128)(2,1)} %copy-done) | copy-start | bytes 5505028
  129.3 26.8 %copy-start.4 = (f32[8,1,64,256]{3,2,1,0:T(8,128)S(1)}, f32[8,1,64,256]{3,2,1,0:T(8,128)}, u32[]{:S(2)}) copy-start(f32[8,1,64,256]{3,2,1,0:T(8,128)} %param.8) | copy-start | bytes 1572868
Sparse Core Ops, SparseCore 0:
  9.5 53.6 all-gather.1
  130.9 23.9 reduce-scatter.3
where the time goes:
time: 230 us; the launch traced here: 229 us
  local copies, waits for them, and re-layouts  75 us (33%)
  waiting for transfers between devices  69.9 us (30%)
  matrix products  32.5 us (14%)
  other arithmetic  21.3 us (9%)
  between operations  14.2 us (6%)
  starting transfers between devices  9.3 us (4%)
  blocking collectives  6.81 us (3%)
    all_to_all x1, waiting for transfers between devices, body(): lax.all_to_all(grid_rows, 'coef', split_axis=1, concat_axis=0, tiled=True)  45.1 us
    unnamed x3, waiting for transfers between devices  24.8 us
    unnamed x19, local copies, waits for them, and re-layouts  21.5 us
    mul x3, local copies, waits for them, and re-layouts, body(): updated = coefficients - 0.5 * misfit_gradient - 0.5 * reg_grad  16.9 us
    dot_general x1, matrix products, body(): lax.dot_general(lax.all_gather(harmonics, 'coef', axis=0, tiled=True), sl...  13.8 us
    all_to_all x1, other arithmetic, body(): lax.all_to_all(reg_grad, 'coef', split_axis=0, concat_axis=1, tiled=True)  13.6 us
    reshape x1, local copies, waits for them, and re-layouts, build_matrix(): product.astype(jnp.bfloat16)  12 us
    dot_general x1, matrix products, body(): jnp.einsum('qci,qbcy->ybi', system_matrix, backward_half, preferred_eleme...  7.78 us
  transfers between devices with their start and end apart: 4, of which 2 were waited for; matrix products, arithmetic and copies ran while one was open for 18% of the time, Pallas kernels for 0%

commit v1 on v0

--- a/solution.py
+++ b/solution.py
@@ -4,6 +4,13 @@
 from jax.sharding import PartitionSpec as P
 
 NG = 64
+
+
+def exchange_blocks(x, axis, split, join):
+    size = lax.axis_size(axis)
+    blocks = jnp.stack(jnp.split(x, size, axis=split), axis=0)
+    blocks = lax.all_to_all(blocks, axis, split_axis=0, concat_axis=0)
+    return jnp.concatenate(blocks, axis=join)
 
 
 def build_matrix(ray_voxels, ray_weights):
@@ -80,7 +87,7 @@
         preferred_element_type=jnp.float32,
     )
     reg_grad = reg_grad.reshape(width_all, row_span, item_count)
-    reg_grad = lax.all_to_all(reg_grad, "coef", split_axis=0, concat_axis=1, tiled=True)
+    reg_grad = exchange_blocks(reg_grad, "coef", 0, 1)
     reg_grad = reg_grad.reshape(coef_local, layers * NG * NG)
     updated = coefficients - 0.5 * misfit_gradient - 0.5 * reg_grad
     return (updated, residual)

time: 230 us -> 187 us (0.81)
  local copies, waits for them, and re-layouts: 75 us -> 41 us
  other arithmetic: 21.3 us -> 12.4 us
    unnamed x19, local copies, waits for them, and re-layouts: 21.5 us -> 5.32 us
    all_to_all x1 -> x0, other arithmetic: 13.6 us -> none  [body(): lax.all_to_all(reg_grad, 'coef', split_axis=0, concat_axis=1, tiled=True)]
    mul x3 -> x1, local copies, waits for them, and re-layouts: 16.9 us -> 5.46 us  [body(): updated = coefficients - 0.5 * misfit_gradient - 0.5 * reg_grad]
    split x0 -> x5, local copies, waits for them, and re-layouts: none -> 8.31 us  [exchange_blocks(): blocks = jnp.stack(jnp.split(x, size, axis=split), axis=0)]
    reshape x1 -> x0, local copies, waits for them, and re-layouts: 7.65 us -> none  [body(): reg_grad = reg_grad.reshape(width_all, row_span, item_count)]
    all_to_all x2 -> x0, local copies, waits for them, and re-layouts: 7.07 us -> none  [body(): lax.all_to_all(reg_grad, 'coef', split_axis=0, concat_axis=1, tiled=True)]
    another operation x0 -> x1, other arithmetic: none -> 3.55 us  [exchange_blocks(): blocks = jnp.stack(jnp.split(x, size, axis=split), axis=0)]
  transfers between devices with their start and end apart: 4 -> 4, of which waited for: 2 -> 2; matrix products, arithmetic and copies ran while one was open for 18% -> 23% of each run, Pallas kernels for 0% -> 0%
where the time goes in v1:
time: 187 us; the launch traced here: 186 us
  waiting for transfers between devices  69.6 us (37%)
  local copies, waits for them, and re-layouts  41 us (22%)
  matrix products  32 us (17%)
  between operations  14.2 us (8%)
  other arithmetic  12.4 us (7%)
  starting transfers between devices  9.55 us (5%)
  blocking collectives  6.83 us (4%)
    all_to_all x1, waiting for transfers between devices, body(): lax.all_to_all(grid_rows, 'coef', split_axis=1, concat_axis=0, tiled=True)  44.4 us
    unnamed x3, waiting for transfers between devices  25.2 us
    dot_general x1, matrix products, body(): lax.dot_general(lax.all_gather(harmonics, 'coef', axis=0, tiled=True), sl...  13.3 us
    reshape x1, local copies, waits for them, and re-layouts, build_matrix(): product.astype(jnp.bfloat16)  12.1 us
    split x5, local copies, waits for them, and re-layouts, exchange_blocks(): blocks = jnp.stack(jnp.split(x, size, axis=split), axis=0)  8.31 us
    dot_general x1, matrix products, body(): jnp.einsum('qci,qbcy->ybi', system_matrix, backward_half, preferred_eleme...  7.78 us
    all_gather x1, blocking collectives, body(): lax.all_gather(resid_half, 'coef', axis=3, tiled=True)  6.83 us
    dot_general x1, matrix products, build_matrix(): lax.dot_general(high_flat, low_flat, (((1,), (1,)), ((0,), (0,))), prefer...  6.66 us
  transfers between devices with their start and end apart: 4, of which 2 were waited for; matrix products, arithmetic and copies ran while one was open for 23% of the time, Pallas kernels for 0%

profile of v1, /device:TPU:0, one launch (start us, length us, event | category | flops | bytes accessed | tf_op | source)
XLA Modules:
  0.0 185.6 jit_solution(11721875421787156479)
XLA Ops:
  7.2 0.0 all-gather.2.cloned.1.call-start
  7.2 0.7 all-gather.2.cloned.1.call-update
  7.9 2.3 %convert_element_type.36 = bf16[224,4096]{1,0:T(8,128)(2,1)S(1)} convert(f32[224,4096]{1,0:T(8,128)} %param.7) | non-fusion elementwise | flops 917504 | bytes 5505024 | tf_op jit(solution)/shard_map/convert_element_type | solution.py:48
  10.2 0.0 copy-start
  10.2 0.0 copy-start.4
  10.2 0.0 copy-start.2
  10.2 2.5 %copy.45 = bf16[224,4096]{0,1:T(8,128)(2,1)} copy(bf16[224,4096]{1,0:T(8,128)(2,1)S(1)} %convert_element_type.36) | data formatting | bytes 3670016 | tf_op jit(solution)/shard_map/convert_element_type | solution.py:48
  12.7 0.0 copy-done
  12.7 4.2 %all-to-all-start = ((bf16[224,64,64]{0,2,1:T(8,128)(2,1)}), bf16[224,64,64]{0,2,1:T(8,128)(2,1)S(1)}, u32[]{:S(2)}, u32[]{:S(2)}) async-start(bf16[224,64,64]{0,2,1:T(8,128)(2,1)} %bitcast.59), calls=%async_computation | async-start | bytes 4194304 | tf_op jit(solution)/shard_map/all_to_all | solution.py:73
  16.9 0.0 copy-done.4
  17.0 0.0 copy-done.2
  17.0 0.9 add_select_fusion.1
  17.9 44.4 %all-to-all-done = bf16[224,64,64]{0,2,1:T(8,128)(2,1)S(1)} async-done(((bf16[224,64,64]{0,2,1:T(8,128)(2,1)}), bf16[224,64,64]{0,2,1:T(8,128)(2,1)S(1)}, u32[]{:S(2)}, u32[]{:S(2)}) %all-to-all-start) | async-done | bytes 1835040 | tf_op jit(solution)/shard_map/all_to_all | solution.py:73
  62.3 3.1 %copy.62 = bf16[224,4,16,64]{0,1,3,2:T(4,128)(2,1)} copy(bf16[224,4,16,64]{0,3,2,1:T(8,128)(2,1)S(1)} %bitcast.58) | data formatting | bytes 3670016 | tf_op jit(solution)/shard_map/all_to_all | solution.py:73
  65.3 3.9 %reshape.65 = bf16[896,1024]{0,1:T(8,128)(2,1)S(1)} reshape(bf16[4,224,16,64]{1,0,3,2:T(4,128)(2,1)} %bitcast.60) | data formatting | bytes 3670016 | tf_op jit(solution)/shard_map/reshape | solution.py:75
  69.3 0.0 all-gather.2.cloned.1.call-done
  69.3 13.3 %fusion.14 = f32[896,1024]{1,0:T(8,128)} fusion(bf16[896,2048]{1,0:T(8,128)(2,1)} %all-gather.2.cloned.1.call-done, bf16[896,1024]{0,1:T(8,128)(2,1)S(1)} %reshape.65), kind=kOutput, calls=%fused_computation.19 | convolution fusion | flops 7524581376 | bytes 9175040 | tf_op jit(solution)/shard_map/dot_general | solution.py:83
  82.6 3.7 %fusion.34 = (f32[224,1024]{1,0:T(8,128)}, f32[224,1024]{1,0:T(8,128)S(1)}, f32[224,1024]{1,0:T(8,128)S(1)}, f32[224,1024]{1,0:T(8,128)}) fusion(f32[896,1024]{1,0:T(8,128)} %fusion.14), kind=kLoop, calls=%fused_computation.44 | loop fusion | bytes 7340032 | tf_op jit(solution)/shard_map/split | solution.py:11
  86.2 0.3 copy.50
  86.6 0.3 copy.49
  86.9 1.5 copy.48
  88.4 2.5 %copy.47 = f32[224,1024]{0,1:T(8,128)} copy(f32[224,1024]{1,0:T(8,128)} %get-tuple-element.10) | data formatting | bytes 1835008 | tf_op jit(solution)/shard_map/split | solution.py:11
  90.9 3.5 %pad_maximum_fusion = f32[4,224,16,64]{1,3,2,0:T(8,128)} fusion(f32[1,224,16,64]{1,3,2,0:T(8,128)S(1)} %bitcast.63, f32[1,224,16,64]{1,3,2,0:T(8,128)S(1)} %bitcast.64, f32[1,224,16,64]{1,3,2,0:T(8,128)S(1)} %bitcast.65, f32[1,224,16,64]{1,3,2,0:T(8,128)} %bitcast.66), kind=kLoop, calls=%fused_computation.13 | loop fusion | flops 2752512 | bytes 7340032 | tf_op jit(solution)/shard_map/stack | solution.py:11
  94.4 0.0 copy-start.3
  94.4 5.1 %all-to-all-start.1 = ((f32[4,224,16,64]{1,3,2,0:T(8,128)}), f32[4,224,16,64]{1,3,2,0:T(8,128)}, u32[]{:S(2)}, u32[]{:S(2)}) async-start(f32[4,224,16,64]{1,3,2,0:T(8,128)} %pad_maximum_fusion), calls=%async_computation.1 | async-start | bytes 8388608 | tf_op jit(solution)/shard_map/all_to_all | solution.py:12
  99.5 0.2 reduce-scatter.4.cloned.1.call-start
  99.7 0.0 copy-done.3
  99.7 6.7 %fusion.5 = bf16[512,64,64]{2,1,0:T(8,128)(2,1)} fusion(s32[512,128]{1,0:T(8,128)S(1)} %bitcast.72, s32[512,128]{1,0:T(8,128)S(1)} %bitcast.71, bf16[512,128]{1,0:T(8,128)(2,1)S(1)} %bitcast.74), kind=kOutput, calls=%fused_computation.8 | convolution fusion | flops 551550976 | bytes 4849664 | tf_op jit(solution)/shard_map/dot_general | solution.py:29
  106.4 0.0 copy-start.6
  106.4 12.1 %reshape.60 = bf16[8,64,4096]{2,1,0:T(8,128)(2,1)} reshape(bf16[512,64,64]{2,1,0:T(8,128)(2,1)} %fusion.5) | data formatting | bytes 8388608 | tf_op jit(solution)/shard_map/reshape | solution.py:32
  118.5 0.0 copy-start.1
  118.5 2.7 %copy.55 = bf16[2,8,224,256]{3,1,2,0:T(8,128)(2,1)S(1)} copy(bf16[2,8,224,256]{3,2,1,0:T(8,128)(2,1)} %bitcast.69) | data formatting | bytes 3670016
  121.1 0.0 copy-done.6
  121.1 0.5 convolution_convert_fusion
  121.6 0.0 copy-done.1
  121.6 3.8 %convolution_bitcast_fusion.1 = f32[8,1,64,256]{3,2,0,1:T(8,128)S(1)} fusion(bf16[8,224,256]{2,0,1:T(8,128)(2,1)S(1)} %bitcast.67, bf16[8,64,4096]{2,1,0:T(8,128)(2,1)} %reshape.60, bf16[224,4096]{1,0:T(8,128)(2,1)S(1)} %copy-done.1), kind=kOutput, calls=%fused_computation.22 | convolution fusion | flops 998359040 | bytes 7471104 | tf_op jit(solution)/shard_map/azrk,akc->azrc/dot_general | solution.py:53
  125.4 0.0 copy-start.5
  125.5 0.4 copy.53
  125.9 1.1 reshape.68
  126.9 0.0 reduce-scatter.4.cloned.1.call-update
  127.0 24.5 %reduce-scatter.4.cloned.1.call-done = f32[64,512]{1,0:T(8,128)} async-done(((f32[256,512]{1,0:T(8,128)}), f32[64,512]{1,0:T(8,128)}) %reduce-scatter.4.cloned.1.call-update) | async-done | bytes 131088
  151.4 1.0 reshape.69
  152.4 0.1 copy.54
  152.6 0.0 copy-done.5
  152.6 0.8 fusion.29
  153.4 0.1 copy.42
  153.6 6.8 %all_gather.7 = bf16[8,1,64,256]{2,0,1,3:T(8,128)(2,1)S(1)} all-gather(bf16[8,1,64,64]{2,0,1,3:T(8,128)(2,1)S(1)} %copy.42), channel_id=1, replica_groups=mesh['groups'=2,'coef'=4,'slab'=4] {'coef'}, dimensions={3}, use_global_device_ids=true | all-gather | bytes 327680 | tf_op jit(solution)/shard_map/all_gather | solution.py:63
  160.4 0.3 copy.43
  160.7 0.0 all-to-all-done.1
  160.8 4.7 %broadcast_multiply_fusion = f32[4,224,16,64]{1,3,2,0:T(8,128)} fusion(f32[4,224,16,64]{1,3,2,0:T(8,128)} %all-to-all-done.1), kind=kLoop, calls=%fused_computation.18 | loop fusion | flops 917504 | bytes 7340032 | tf_op jit(solution)/shard_map/mul | solution.py:92
  165.5 5.5 %copy.51 = f32[224,4096]{1,0:T(8,128)} copy(f32[224,4096]{0,1:T(8,128)} %bitcast.57) | data formatting | bytes 7340032 | tf_op jit(solution)/shard_map/mul | solution.py:92
  171.0 7.8 %fusion.10 = f32[224,4096]{1,0:T(8,128)} fusion(f32[224,4096]{1,0:T(8,128)} %copy.51, f32[224,4096]{1,0:T(8,128)} %param.7, bf16[8,64,4096]{2,1,0:T(8,128)(2,1)} %reshape.60, bf16[8,224,256]{2,0,1:T(8,128)(2,1)S(1)} %bitcast.68, bf16[8,1,64,256]{3,2,0,1:T(8,128)(2,1)S(1)} %copy.43), kind=kOutput, calls=%fused_computation.12 | convolution fusion | flops 1001111552 | bytes 16384000 | tf_op jit(solution)/shard_map/qci,qbcy->ybi/dot_general | solution.py:68
  (1 shorter events, 0.0 us)
Async XLA Ops:
  7.2 62.1 %all-gather.2.cloned.1.call-start = ((), (), s32[]{:S(2)}) async-start(), calls=%async_computation.3 | async-start | bytes 4587520 | tf_op jit(solution)/shard_map/all_gather | solution.py:84
  10.2 2.5 %copy-start = (bf16[224,4096]{1,0:T(8,128)(2,1)}, bf16[224,4096]{1,0:T(8,128)(2,1)S(1)}, u32[]{:S(2)}) copy-start(bf16[224,4096]{1,0:T(8,128)(2,1)S(1)} %convert_element_type.36) | copy-start | bytes 5505028
  10.2 6.7 %copy-start.4 = (s32[8,64,128]{2,1,0:T(8,128)S(1)}, s32[8,64,128]{2,1,0:T(8,128)}, u32[]{:S(2)}) copy-start(s32[8,64,128]{2,1,0:T(8,128)} %param.10) | copy-start | bytes 786436
  10.2 6.8 %copy-start.2 = (s32[8,64,128]{2,1,0:T(8,128)S(1)}, s32[8,64,128]{2,1,0:T(8,128)}, u32[]{:S(2)}) copy-start(s32[8,64,128]{2,1,0:T(8,128)} %param.9) | copy-start | bytes 786436
  12.7 49.6 %all-to-all-start = ((bf16[224,64,64]{0,2,1:T(8,128)(2,1)}), bf16[224,64,64]{0,2,1:T(8,128)(2,1)S(1)}, u32[]{:S(2)}, u32[]{:S(2)}) async-start(bf16[224,64,64]{0,2,1:T(8,128)(2,1)} %bitcast.59), calls=%async_computation | async-start | bytes 4194304 | tf_op jit(solution)/shard_map/all_to_all | solution.py:73
  94.4 5.3 %copy-start.3 = (s32[8,64,128]{2,1,0:T(8,128)S(1)}, s32[8,64,128]{2,1,0:T(8,128)}, u32[]{:S(2)}) copy-start(s32[8,64,128]{2,1,0:T(8,128)} %get-tuple-element.17) | copy-start | bytes 786436
  94.4 66.3 %all-to-all-start.1 = ((f32[4,224,16,64]{1,3,2,0:T(8,128)}), f32[4,224,16,64]{1,3,2,0:T(8,128)}, u32[]{:S(2)}, u32[]{:S(2)}) async-start(f32[4,224,16,64]{1,3,2,0:T(8,128)} %pad_maximum_fusion), calls=%async_computation.1 | async-start | bytes 8388608 | tf_op jit(solution)/shard_map/all_to_all | solution.py:12
  99.5 51.9 %reduce-scatter.4.cloned.1.call-start = ((), (), s32[]{:S(2)}) async-start(), calls=%async_computation.4 | async-start | bytes 655360
  106.4 14.7 %copy-start.6 = (s32[8]{0:T(128)S(1)}, s32[8]{0:T(128)}, u32[]{:S(2)}) copy-start(s32[8]{0:T(128)} %param.11) | copy-start | bytes 100
  118.5 3.1 %copy-start.1 = (bf16[224,4096]{1,0:T(8,128)(2,1)S(1)}, bf16[224,4096]{1,0:T(8,128)(2,1)}, u32[]{:S(2)}) copy-start(bf16[224,4096]{1,0:T(8,128)(2,1)} %copy-done) | copy-start | bytes 5505028
  125.4 27.1 %copy-start.5 = (f32[8,1,64,256]{3,2,1,0:T(8,128)S(1)}, f32[8,1,64,256]{3,2,1,0:T(8,128)}, u32[]{:S(2)}) copy-start(f32[8,1,64,256]{3,2,1,0:T(8,128)} %param.8) | copy-start | bytes 1572868
Sparse Core Ops, SparseCore 0:
  9.5 53.6 all-gather.1
  127.1 24.3 reduce-scatter.3
